TPU v7x, 32 devices: a whole 2x2x4 slice. The times are simulated.
32 devices in a mesh: layer: 4 (over y, x), row: 2 (over core), col: 4 (over z).
Axes of the slice: x: 2, y: 2, z: 4, core: 2. Of those that a mesh axis runs over, the one named last changes fastest.
Arguments:
- blocks: bfloat16 [13, 512, 128, 128], P(None, ('row', 'col'), 'layer'), may hold values from -0.29882812 to 0.29882812
- presence: int32 [13, 512], P(None, ('row', 'col')), may hold values from 0 to 1, as said below
Outputs:
- purified: bfloat16 [13, 512, 128, 128], P(None, ('row', 'col'), 'layer')
Inputs may be any that keep to these rules, and one draw needn't show every extreme that they name: `presence`: the tile on offset 0 is present in every block row.
All inputs are finite; a program needn't handle non-finite values.
Results may differ from a plain program's by a relative error of at most 0.01.
Values may be sent and summed in bfloat16 or wider, within the bound.
A program may use at most 320 MiB of HBM per device.

v0:
```python
import jax
import jax.numpy as jnp
import numpy as np
from jax import lax
from jax.sharding import PartitionSpec as P

NBG = 512
BAND = 3
FAR = 160


def passed_along(block, axis, distance):
    devices = range(lax.axis_size(axis))
    route = [((i - distance) % len(devices), i) for i in devices]
    return lax.ppermute(block, axis, route)


def with_halo(block, sides, width):
    for axis, dim in sides:
        count = lax.axis_size(axis)
        forward = [(i, i + 1) for i in range(count - 1)]
        forward.append((count - 1, 0))
        backward = [(target, source) for source, target in forward]
        low = lax.ppermute(
            lax.slice_in_dim(block, block.shape[dim] - width, None, axis=dim), axis, forward
        )
        high = lax.ppermute(lax.slice_in_dim(block, 0, width, axis=dim), axis, backward)
        block = jnp.concatenate([low, block, high], axis=dim)
    return block


def offset_table():
    values = list(range(-BAND, BAND + 1))
    values = values + [FAR - 1, FAR, FAR + 1, -FAR - 1, -FAR, -FAR + 1]
    return [value % NBG for value in values]


def pair_table(offsets):
    by_target = []
    for target_index in range(len(offsets)):
        entries = []
        for left_index in range(len(offsets)):
            for right_index in range(len(offsets)):
                if (offsets[left_index] + offsets[right_index]) % NBG == offsets[target_index]:
                    entries.append((left_index, right_index))
        by_target.append(entries)
    return by_target


def fetch_far(source, offset, groups, local_rows):
    whole_steps, remainder = divmod(offset, local_rows)
    upper = passed_along(source[:, remainder:], ("row", "col"), -whole_steps % groups)
    if remainder == 0:
        return upper
    lower = passed_along(source[:, :remainder], ("row", "col"), (-whole_steps - 1) % groups)
    return jnp.concatenate([upper, lower], axis=1)


def per_device(blocks, presence):
    groups = lax.axis_size(("row", "col"))
    local_rows = blocks.shape[1]
    offsets = offset_table()
    by_target = pair_table(offsets)
    weight_mask = presence.astype(jnp.float32)[:, :, None, None]
    masked = blocks * presence.astype(jnp.bfloat16)[:, :, None, None]
    padded = with_halo(masked, ((("row", "col"), 1),), BAND)
    far_windows = {}
    for left_index in range(2 * BAND + 1, len(offsets)):
        needed = sorted(
            set(
                (
                    entry[1]
                    for target_list in by_target
                    for entry in target_list
                    if entry[0] == left_index
                )
            )
        )
        picked = jnp.take(masked, np.array(needed), axis=0)
        far_windows[left_index] = (
            fetch_far(picked, offsets[left_index], groups, local_rows),
            needed,
        )

    def right_piece(left_index, right_index):
        if left_index <= 2 * BAND:
            return padded[right_index, left_index : left_index + local_rows]
        window, needed = far_windows[left_index]
        return window[needed.index(right_index)]

    def product(left_tiles):
        totals = []
        for target_index in range(len(offsets)):
            pairs = by_target[target_index]
            lefts = jnp.concatenate(
                [left_tiles[left_index] for left_index, right_index in pairs], axis=2
            )
            rights = jnp.concatenate(
                [right_piece(left_index, right_index) for left_index, right_index in pairs], axis=1
            )
            totals.append(
                jnp.einsum("ixk,iky->ixy", lefts, rights, preferred_element_type=jnp.float32)
            )
        return jnp.stack(totals)

    left_first = lax.all_to_all(masked, "layer", split_axis=3, concat_axis=2, tiled=True)
    second = (
        lax.psum_scatter(product(left_first), "layer", scatter_dimension=2, tiled=True)
        * weight_mask
    ).astype(jnp.bfloat16)
    left_second = lax.all_to_all(second, "layer", split_axis=3, concat_axis=2, tiled=True)
    third = (
        lax.psum_scatter(
            product(left_second).astype(jnp.bfloat16), "layer", scatter_dimension=2, tiled=True
        ).astype(jnp.float32)
        * weight_mask
    )
    return (3.0 * second.astype(jnp.float32) - 2.0 * third).astype(jnp.bfloat16)


def solution(mesh):
    placed = (P(None, ("row", "col"), "layer", None), P(None, ("row", "col")))
    return jax.shard_map(
        per_device,
        mesh=mesh,
        in_specs=placed,
        out_specs=P(None, ("row", "col"), "layer", None),
        check_vma=False,
    )
```

profile of v0, /device:TPU:0, one launch (start us, length us, event | category | flops | bytes accessed | tf_op | source)
XLA Modules:
  0.0 2231.8 jit_solution(13494582447131702137)
XLA Ops:
  7.9 6.6 broadcast_multiply_fusion
  14.5 24.0 %copy.159 = bf16[13,64,32,128]{1,2,0,3:T(8,128)(2,1)} copy(bf16[13,64,32,128]{3,2,1,0:T(8,128)(2,1)} %broadcast_multiply_fusion) | data formatting | bytes 13631488 | tf_op jit(solution)/shard_map/mul | solution.py:65
  38.5 13.8 reshape.119
  52.3 5.5 all-to-all-start
  79.5 5.6 gather_fusion.5
  105.4 5.9 gather_fusion
  134.3 111.9 %collective-permute-done.10 = bf16[6,31,32,128]{3,2,1,0:T(8,128)(2,1)} collective-permute-done((bf16[6,31,32,128]{3,2,1,0:T(8,128)(2,1)}, bf16[6,31,32,128]{3,2,1,0:T(8,128)(2,1)}, u32[]{:S(2)}, u32[]{:S(2)}) %collective-permute-start.10) | collective-permute-done | bytes 1523744 | tf_op jit(solution)/shard_map/ppermute | solution.py:15
  246.2 32.9 %collective-permute-start.4 = (bf16[6,33,32,128]{3,2,1,0:T(8,128)(2,1)S(1)}, bf16[6,33,32,128]{3,2,1,0:T(8,128)(2,1)S(1)}, u32[]{:S(2)}, u32[]{:S(2)}) collective-permute-start(bf16[6,33,32,128]{3,2,1,0:T(8,128)(2,1)S(1)} %copy-done.32), channel_id=1, source_target_pairs={{5,0},{6,1},{7,2},{0,3},{1,4},{2,5},{3,6},{4,7},{13,8},{14,9},{15,... | collective-permute-start | bytes 4866056 | tf_op jit(solution)/shard_map/ppermute | solution.py:15
  294.4 120.7 %collective-permute-start.2 = (bf16[6,33,32,128]{3,2,1,0:T(8,128)(2,1)S(1)}, bf16[6,33,32,128]{3,2,1,0:T(8,128)(2,1)}, u32[]{:S(2)}, u32[]{:S(2)}) collective-permute-start(bf16[6,33,32,128]{3,2,1,0:T(8,128)(2,1)S(1)} %slice.876), channel_id=1, source_target_pairs={{2,0},{3,1},{4,2},{5,3},{6,4},{7,5},{0,6},{1,7},{10,8},{11,9},{12,... | collective-permute-start | bytes 4866056 | tf_op jit(solution)/shard_map/ppermute | solution.py:15
  417.0 97.6 %collective-permute-done.9 = bf16[6,32,32,128]{3,2,1,0:T(8,128)(2,1)S(1)} collective-permute-done((bf16[6,32,32,128]{3,2,1,0:T(8,128)(2,1)S(1)}, bf16[6,32,32,128]{3,2,1,0:T(8,128)(2,1)S(1)}, u32[]{:S(2)}, u32[]{:S(2)}) %collective-permute-start.9) | collective-permute-done | bytes 1572896 | tf_op jit(solution)/shard_map/ppermute | solution.py:15
  523.1 93.8 %collective-permute-done.5 = bf16[6,31,32,128]{3,2,1,0:T(8,128)(2,1)} collective-permute-done((bf16[6,31,32,128]{3,2,1,0:T(8,128)(2,1)}, bf16[6,31,32,128]{3,2,1,0:T(8,128)(2,1)}, u32[]{:S(2)}, u32[]{:S(2)}) %collective-permute-start.5) | collective-permute-done | bytes 1523744 | tf_op jit(solution)/shard_map/ppermute | solution.py:15
  618.6 33.1 %collective-permute-done.2 = bf16[6,33,32,128]{3,2,1,0:T(8,128)(2,1)} collective-permute-done((bf16[6,33,32,128]{3,2,1,0:T(8,128)(2,1)S(1)}, bf16[6,33,32,128]{3,2,1,0:T(8,128)(2,1)}, u32[]{:S(2)}, u32[]{:S(2)}) %collective-permute-start.2) | collective-permute-done | bytes 1622048 | tf_op jit(solution)/shard_map/ppermute | solution.py:15
  655.7 30.6 %collective-permute-done.13 = bf16[6,33,32,128]{3,2,1,0:T(8,128)(2,1)S(1)} collective-permute-done((bf16[6,33,32,128]{3,2,1,0:T(8,128)(2,1)S(1)}, bf16[6,33,32,128]{3,2,1,0:T(8,128)(2,1)S(1)}, u32[]{:S(2)}, u32[]{:S(2)}) %collective-permute-start.13) | collective-permute-done | bytes 1622048 | tf_op jit(solution)/shard_map/ppermute | solution.py:15
  701.1 13.7 reshape.120
  714.8 13.1 copy.160
  746.8 4.9 copy.161
  756.6 5.1 copy.166
  795.0 15.4 concatenate.198
  810.4 21.3 concatenate.203
  831.7 26.5 %concatenate.207 = bf16[64,128,416]{2,1,0:T(8,128)(2,1)} concatenate(bf16[64,128,32]{2,1,0:T(8,128)(2,1)} %bitcast.600, bf16[64,128,32]{2,1,0:T(8,128)(2,1)} %bitcast.496, bf16[64,128,32]{2,1,0:T(8,128)(2,1)} %bitcast.472, bf16[64,128,32]{2,1,0:T(8,128)(2,1)S(1)} %bitcast.429, bf16[64,128,32]{2,1,0:T(8,128)(2,1)} %bitcast.452, bf16[64,128,32]{2,1,0:T(8,128)(2,1)} %bitcast.488, ...), dimensions={2} | concatenate | bytes 13631488 | tf_op jit(solution)/shard_map/concatenate | solution.py:95
  858.2 21.3 concatenate.211
  879.5 15.5 concatenate.213
  895.0 13.6 concatenate.217
  908.6 13.2 concatenate.219
  921.8 13.2 concatenate.221
  935.0 13.2 concatenate.223
  948.1 13.2 concatenate.225
  961.3 13.3 concatenate.227
  974.6 8.0 bitcast_dynamic-update-slice_fusion.12
  982.5 5.5 bitcast_dynamic-update-slice_fusion.11
  988.0 8.3 bitcast_dynamic-update-slice_fusion.10
  996.3 7.4 bitcast_dynamic-update-slice_fusion.9
  1003.7 6.4 bitcast_dynamic-update-slice_fusion.8
  1010.2 5.5 bitcast_dynamic-update-slice_fusion.7
  1032.8 5.4 bitcast_dynamic-update-slice_fusion.2
  1038.2 5.2 bitcast_dynamic-update-slice_fusion.1
  1043.4 5.1 bitcast_dynamic-update-slice_fusion
  1048.6 457.3 %reduce-scatter.3.cloned.1.call-done = f32[13,64,32,128]{3,2,1,0:T(8,128)} async-done(((f32[13,64,128,128]{3,2,1,0:T(8,128)}), f32[13,64,32,128]{3,2,1,0:T(8,128)}) %reduce-scatter.3.cloned.1.call-update) | async-done | bytes 13631504 | tf_op jit(solution)/shard_map/reduce_scatter | solution.py:108
  1505.9 8.1 multiply_convert_fusion
  1514.0 24.0 %copy.185 = bf16[13,64,32,128]{1,2,0,3:T(8,128)(2,1)} copy(bf16[13,64,32,128]{3,2,1,0:T(8,128)(2,1)} %multiply_convert_fusion) | data formatting | bytes 13631488 | tf_op jit(solution)/shard_map/convert_element_type | solution.py:110
  1538.1 13.8 reshape.121
  1551.9 83.3 %all_to_all.30 = bf16[4,2,425984]{2,1,0:T(2,128)(2,1)} all-to-all(bf16[4,2,425984]{2,1,0:T(2,128)(2,1)} %reshape.121), channel_id=1, replica_groups=mesh['layer'=4,'row'=2,'col'=4] {'layer'}, dimensions={0} | all-to-all | bytes 13631488 | tf_op jit(solution)/shard_map/all_to_all | solution.py:111
  1635.2 13.5 reshape.122
  1648.7 13.1 copy.186
  1690.5 5.1 copy.192
  1700.4 4.9 copy.195
  1728.8 7.4 bitcast_dynamic-update-slice_fusion.25
  1736.3 15.4 concatenate.230
  1751.7 21.3 concatenate.231
  1773.0 26.5 %concatenate.232 = bf16[64,128,416]{2,1,0:T(8,128)(2,1)} concatenate(bf16[64,128,32]{2,1,0:T(8,128)(2,1)} %bitcast.605, bf16[64,128,32]{2,1,0:T(8,128)(2,1)} %bitcast.504, bf16[64,128,32]{2,1,0:T(8,128)(2,1)} %bitcast.463, bf16[64,128,32]{2,1,0:T(8,128)(2,1)S(1)} %bitcast.417, bf16[64,128,32]{2,1,0:T(8,128)(2,1)} %bitcast.442, bf16[64,128,32]{2,1,0:T(8,128)(2,1)} %bitcast.481, ...), dimensions={2} | concatenate | bytes 13631488 | tf_op jit(solution)/shard_map/concatenate | solution.py:95
  1799.5 21.3 concatenate.233
  1820.8 15.5 concatenate.234
  1836.3 13.2 concatenate.236
  1849.5 13.2 concatenate.237
  1862.7 13.2 concatenate.238
  1875.9 13.2 concatenate.239
  1889.0 13.2 concatenate.240
  1902.2 13.4 concatenate.241
  1915.6 6.0 bitcast_dynamic-update-slice_fusion.24
  1921.7 7.6 bitcast_dynamic-update-slice_fusion.23
  1929.2 6.9 bitcast_dynamic-update-slice_fusion.22
  1936.2 5.8 bitcast_dynamic-update-slice_fusion.21
  1975.5 238.3 %reduce-scatter.5.cloned.1.call-done = bf16[13,64,32,128]{3,2,1,0:T(8,128)(2,1)} async-done(((bf16[13,64,128,128]{3,2,1,0:T(8,128)(2,1)}), bf16[13,64,32,128]{3,2,1,0:T(8,128)(2,1)}) %reduce-scatter.5.cloned.1.call-update) | async-done | bytes 6815760 | tf_op jit(solution)/shard_map/reduce_scatter | solution.py:113
  2213.9 10.7 subtract_convert_fusion
  (256 shorter events, 277.0 us)
Async XLA Ops:
  52.3 12.0 copy-start.58
  52.3 12.0 copy-start.59
  52.3 648.8 %all-to-all-start = ((bf16[4,2,425984]{2,1,0:T(2,128)(2,1)}), bf16[4,2,425984]{2,1,0:T(2,128)(2,1)}, u32[]{:S(2)}, u32[]{:S(2)}) async-start(bf16[4,2,425984]{2,1,0:T(2,128)(2,1)} %reshape.119), calls=%async_computation | async-start | bytes 13631488 | tf_op jit(solution)/shard_map/all_to_all | solution.py:106
  57.7 1448.2 %reduce-scatter.3.cloned.1.call-start = ((), (), s32[]{:S(2)}) async-start(), calls=%async_computation.4 | async-start | bytes 68157440 | tf_op jit(solution)/shard_map/reduce_scatter | solution.py:108
  59.7 67.6 %collective-permute-start.1 = (bf16[13,3,32,128]{3,2,1,0:T(8,128)(2,1)}, bf16[13,3,32,128]{3,2,1,0:T(8,128)(2,1)S(1)}, u32[]{:S(2)}, u32[]{:S(2)}) collective-permute-start(bf16[13,3,32,128]{3,2,1,0:T(8,128)(2,1)} %get-tuple-element.88), channel_id=1, source_target_pairs={{1,0},{2,1},{3,2},{4,3},{5,4},{6,5},{7,6},{0,7},{9,8},{10,9},{11,1... | collective-permute-start | bytes 958472 | tf_op jit(solution)/shard_map/ppermute | solution.py:27
  64.3 54.9 %collective-permute-start = (bf16[13,3,32,128]{3,2,1,0:T(8,128)(2,1)}, bf16[13,3,32,128]{3,2,1,0:T(8,128)(2,1)}, u32[]{:S(2)}, u32[]{:S(2)}) collective-permute-start(bf16[13,3,32,128]{3,2,1,0:T(8,128)(2,1)} %get-tuple-element.89), channel_id=1, source_target_pairs={{0,1},{1,2},{2,3},{3,4},{4,5},{5,6},{6,7},{7,0},{8,9},{9,10},{10,1... | collective-permute-start | bytes 958472 | tf_op jit(solution)/shard_map/ppermute | solution.py:24
  70.8 216.8 %collective-permute-start.6 = (bf16[6,32,32,128]{3,2,1,0:T(8,128)(2,1)}, bf16[6,32,32,128]{3,2,1,0:T(8,128)(2,1)}, u32[]{:S(2)}, u32[]{:S(2)}) collective-permute-start(bf16[6,32,32,128]{3,2,1,0:T(8,128)(2,1)} %get-tuple-element.129), channel_id=1, source_target_pairs={{2,0},{3,1},{4,2},{5,3},{6,4},{7,5},{0,6},{1,7},{10,8},{11,9},{12,... | collective-permute-start | bytes 4718600 | tf_op jit(solution)/shard_map/ppermute | solution.py:15
  75.3 9.9 copy-start.30
  77.1 169.1 %collective-permute-start.10 = (bf16[6,31,32,128]{3,2,1,0:T(8,128)(2,1)}, bf16[6,31,32,128]{3,2,1,0:T(8,128)(2,1)}, u32[]{:S(2)}, u32[]{:S(2)}) collective-permute-start(bf16[6,31,32,128]{3,2,1,0:T(8,128)(2,1)} %slice.922), channel_id=1, source_target_pairs={{2,0},{3,1},{4,2},{5,3},{6,4},{7,5},{0,6},{1,7},{10,8},{11,9},{12,... | collective-permute-start | bytes 4571144 | tf_op jit(solution)/shard_map/ppermute | solution.py:15
  88.0 191.1 %collective-permute-start.12 = (bf16[6,31,32,128]{3,2,1,0:T(8,128)(2,1)}, bf16[6,31,32,128]{3,2,1,0:T(8,128)(2,1)}, u32[]{:S(2)}, u32[]{:S(2)}) collective-permute-start(bf16[6,31,32,128]{3,2,1,0:T(8,128)(2,1)} %slice.927), channel_id=1, source_target_pairs={{5,0},{6,1},{7,2},{0,3},{1,4},{2,5},{3,6},{4,7},{13,8},{14,9},{15,... | collective-permute-start | bytes 4571144 | tf_op jit(solution)/shard_map/ppermute | solution.py:15
  105.4 13.0 slice-start
  111.3 6.7 copy-start.31
  111.3 7.1 slice-start.1
  119.2 175.2 %collective-permute-start.7 = (bf16[6,32,32,128]{3,2,1,0:T(8,128)(2,1)S(1)}, bf16[6,32,32,128]{3,2,1,0:T(8,128)(2,1)S(1)}, u32[]{:S(2)}, u32[]{:S(2)}) collective-permute-start(bf16[6,32,32,128]{3,2,1,0:T(8,128)(2,1)S(1)} %copy-done.39), channel_id=1, source_target_pairs={{3,0},{4,1},{5,2},{6,3},{7,4},{0,5},{1,6},{2,7},{11,8},{12,9},{13,... | collective-permute-start | bytes 4718600 | tf_op jit(solution)/shard_map/ppermute | solution.py:15
  127.3 287.8 %collective-permute-start.8 = (bf16[6,32,32,128]{3,2,1,0:T(8,128)(2,1)S(1)}, bf16[6,32,32,128]{3,2,1,0:T(8,128)(2,1)S(1)}, u32[]{:S(2)}, u32[]{:S(2)}) collective-permute-start(bf16[6,32,32,128]{3,2,1,0:T(8,128)(2,1)S(1)} %copy-done.41), channel_id=1, source_target_pairs={{5,0},{6,1},{7,2},{0,3},{1,4},{2,5},{3,6},{4,7},{13,8},{14,9},{15,... | collective-permute-start | bytes 4718600 | tf_op jit(solution)/shard_map/ppermute | solution.py:15
  131.2 115.0 %copy-start.32 = (bf16[6,33,32,128]{3,2,1,0:T(8,128)(2,1)S(1)}, bf16[6,33,32,128]{3,2,1,0:T(8,128)(2,1)}, u32[]{:S(2)}) copy-start(bf16[6,33,32,128]{3,2,1,0:T(8,128)(2,1)} %slice.879) | copy-start | bytes 4866052
  131.2 147.9 %copy-start.40 = (bf16[6,32,32,128]{3,2,1,0:T(8,128)(2,1)S(1)}, bf16[6,32,32,128]{3,2,1,0:T(8,128)(2,1)}, u32[]{:S(2)}) copy-start(bf16[6,32,32,128]{3,2,1,0:T(8,128)(2,1)} %get-tuple-element.126) | copy-start | bytes 4718596
  246.2 269.4 %collective-permute-start.4 = (bf16[6,33,32,128]{3,2,1,0:T(8,128)(2,1)S(1)}, bf16[6,33,32,128]{3,2,1,0:T(8,128)(2,1)S(1)}, u32[]{:S(2)}, u32[]{:S(2)}) collective-permute-start(bf16[6,33,32,128]{3,2,1,0:T(8,128)(2,1)S(1)} %copy-done.32), channel_id=1, source_target_pairs={{5,0},{6,1},{7,2},{0,3},{1,4},{2,5},{3,6},{4,7},{13,8},{14,9},{15,... | collective-permute-start | bytes 4866056 | tf_op jit(solution)/shard_map/ppermute | solution.py:15
  279.1 235.5 %collective-permute-start.9 = (bf16[6,32,32,128]{3,2,1,0:T(8,128)(2,1)S(1)}, bf16[6,32,32,128]{3,2,1,0:T(8,128)(2,1)S(1)}, u32[]{:S(2)}, u32[]{:S(2)}) collective-permute-start(bf16[6,32,32,128]{3,2,1,0:T(8,128)(2,1)S(1)} %copy-done.40), channel_id=1, source_target_pairs={{6,0},{7,1},{0,2},{1,3},{2,4},{3,5},{4,6},{5,7},{14,8},{15,9},{8,1... | collective-permute-start | bytes 4718600 | tf_op jit(solution)/shard_map/ppermute | solution.py:15
  287.6 329.3 %collective-permute-start.5 = (bf16[6,31,32,128]{3,2,1,0:T(8,128)(2,1)}, bf16[6,31,32,128]{3,2,1,0:T(8,128)(2,1)}, u32[]{:S(2)}, u32[]{:S(2)}) collective-permute-start(bf16[6,31,32,128]{3,2,1,0:T(8,128)(2,1)} %slice.880), channel_id=1, source_target_pairs={{6,0},{7,1},{0,2},{1,3},{2,4},{3,5},{4,6},{5,7},{14,8},{15,9},{8,1... | collective-permute-start | bytes 4571144 | tf_op jit(solution)/shard_map/ppermute | solution.py:15
  294.4 122.6 %copy-start.33 = (bf16[6,32,32,128]{3,2,1,0:T(8,128)(2,1)}, bf16[6,32,32,128]{3,2,1,0:T(8,128)(2,1)S(1)}, u32[]{:S(2)}) copy-start(bf16[6,32,32,128]{3,2,1,0:T(8,128)(2,1)S(1)} %collective-permute-done.7) | copy-start | bytes 4718596
  294.4 357.3 %collective-permute-start.2 = (bf16[6,33,32,128]{3,2,1,0:T(8,128)(2,1)S(1)}, bf16[6,33,32,128]{3,2,1,0:T(8,128)(2,1)}, u32[]{:S(2)}, u32[]{:S(2)}) collective-permute-start(bf16[6,33,32,128]{3,2,1,0:T(8,128)(2,1)S(1)} %slice.876), channel_id=1, source_target_pairs={{2,0},{3,1},{4,2},{5,3},{6,4},{7,5},{0,6},{1,7},{10,8},{11,9},{12,... | collective-permute-start | bytes 4866056 | tf_op jit(solution)/shard_map/ppermute | solution.py:15
  415.1 238.4 %collective-permute-start.3 = (bf16[6,31,32,128]{3,2,1,0:T(8,128)(2,1)}, bf16[6,31,32,128]{3,2,1,0:T(8,128)(2,1)}, u32[]{:S(2)}, u32[]{:S(2)}) collective-permute-start(bf16[6,31,32,128]{3,2,1,0:T(8,128)(2,1)} %slice.877), channel_id=1, source_target_pairs={{3,0},{4,1},{5,2},{6,3},{7,4},{0,5},{1,6},{2,7},{11,8},{12,9},{13,... | collective-permute-start | bytes 4571144 | tf_op jit(solution)/shard_map/ppermute | solution.py:15
  514.6 140.6 %collective-permute-start.11 = (bf16[6,33,32,128]{3,2,1,0:T(8,128)(2,1)S(1)}, bf16[6,33,32,128]{3,2,1,0:T(8,128)(2,1)S(1)}, u32[]{:S(2)}, u32[]{:S(2)}) collective-permute-start(bf16[6,33,32,128]{3,2,1,0:T(8,128)(2,1)S(1)} %slice.923), channel_id=1, source_target_pairs={{3,0},{4,1},{5,2},{6,3},{7,4},{0,5},{1,6},{2,7},{11,8},{12,9},{13,... | collective-permute-start | bytes 4866056 | tf_op jit(solution)/shard_map/ppermute | solution.py:15
  515.6 5.9 copy-start.36
  515.6 170.7 %collective-permute-start.13 = (bf16[6,33,32,128]{3,2,1,0:T(8,128)(2,1)S(1)}, bf16[6,33,32,128]{3,2,1,0:T(8,128)(2,1)S(1)}, u32[]{:S(2)}, u32[]{:S(2)}) collective-permute-start(bf16[6,33,32,128]{3,2,1,0:T(8,128)(2,1)S(1)} %slice.928), channel_id=1, source_target_pairs={{6,0},{7,1},{0,2},{1,3},{2,4},{3,5},{4,6},{5,7},{14,8},{15,9},{8,1... | collective-permute-start | bytes 4866056 | tf_op jit(solution)/shard_map/ppermute | solution.py:15
  693.1 5.6 copy-start.21
  693.1 5.6 copy-start.24
  693.1 5.6 copy-start.27
  961.3 13.3 copy-start.50
  961.3 13.3 copy-start.51
  974.6 8.0 copy-start.7
  982.5 13.7 slice-start.2
  988.0 8.3 slice-start.3
  988.0 15.7 slice-start.4
  996.3 7.4 slice-start.5
  1003.7 6.4 copy-start.6
  1010.1 5.6 copy-start.1
  1010.1 5.6 copy-start.3
  1010.1 5.6 copy-start.5
  1010.1 5.6 copy-start.42
  1010.1 5.6 copy-start.44
  1010.2 5.6 copy-start.46
  1010.2 5.6 copy-start.48
  1020.2 4.7 copy-start.25
  1032.8 5.4 copy-start.16
  1038.2 5.2 copy-start.15
  1048.5 457.4 %copy-start.52 = (f32[13,64]{1,0:T(8,128)S(1)}, f32[13,64]{1,0:T(8,128)}, u32[]{:S(2)}) copy-start(f32[13,64]{1,0:T(8,128)} %get-tuple-element.130) | copy-start | bytes 9988
  1048.5 1165.4 %reduce-scatter.5.cloned.1.call-start = ((), (), s32[]{:S(2)}) async-start(), calls=%async_computation.5 | async-start | bytes 34078720 | tf_op jit(solution)/shard_map/reduce_scatter | solution.py:113
  1915.6 13.6 slice-start.8
  1921.7 7.6 slice-start.9
  1921.7 14.5 slice-start.6
  1929.2 6.9 slice-start.7
  1936.2 5.8 copy-start.14
  1942.0 4.9 copy-start
  1942.0 4.9 copy-start.2
  1942.0 4.9 copy-start.4
  1942.0 4.9 copy-start.43
  1942.0 4.9 copy-start.45
  1942.0 4.9 copy-start.47
  1942.0 4.9 copy-start.49
  1961.6 4.7 copy-start.9
  1966.3 4.7 copy-start.8
  1975.5 238.4 %copy-start.53 = (f32[13,64]{1,0:T(8,128)S(1)}, f32[13,64]{1,0:T(8,128)}, u32[]{:S(2)}) copy-start(f32[13,64]{1,0:T(8,128)} %get-tuple-element.130) | copy-start | bytes 9988
  (23 other events, 75.9 us)
Sparse Core Ops, SparseCore 0:
  1048.6 457.2 reduce-scatter.2
  1975.7 238.1 reduce-scatter.4
where the time goes:
time: 2250 us; the launch traced here: 2230 us
  waiting for transfers between devices  1060 us (47%)
  local copies, waits for them, and re-layouts  707 us (31%)
  starting transfers between devices  179 us (8%)
  matrix products  136 us (6%)
  blocking collectives  83.3 us (4%)
  other arithmetic  49.6 us (2%)
    reduce_scatter x1, waiting for transfers between devices, per_device(): lax.psum_scatter(product(left_first), 'layer', scatter_dimension=2, tiled...  457 us
    ppermute x12, waiting for transfers between devices, passed_along(): return lax.ppermute(block, axis, route)  367 us
    concatenate x22, local copies, waits for them, and re-layouts, product(): jnp.concatenate([left_tiles[left_index] for left_index, right_index in pa...  359 us
    reduce_scatter x1, waiting for transfers between devices, per_device(): lax.psum_scatter(product(left_second).astype(jnp.bfloat16), 'layer', scat...  238 us
    ppermute x12, starting transfers between devices, passed_along(): return lax.ppermute(block, axis, route)  169 us
    dot_general x26, matrix products, product(): jnp.einsum('ixk,iky->ixy', lefts, rights, preferred_element_type=jnp.floa...  136 us
    slice x28, local copies, waits for them, and re-layouts, product(): left_tiles[left_index]  134 us
    all_to_all x1, blocking collectives, per_device(): lax.all_to_all(second, 'layer', split_axis=3, concat_axis=2, tiled=True)  83.3 us
  transfers between devices with their start and end apart: 17, of which 7 were waited for; matrix products, arithmetic and copies ran while one was open for 5% of the time, Pallas kernels for 0%

commit v1 on v0

--- a/solution.py
+++ b/solution.py
@@ -108,7 +108,10 @@
         lax.psum_scatter(product(left_first), "layer", scatter_dimension=2, tiled=True)
         * weight_mask
     ).astype(jnp.bfloat16)
-    left_second = lax.all_to_all(second, "layer", split_axis=3, concat_axis=2, tiled=True)
+    left_second = jnp.concatenate(
+        lax.all_to_all(jnp.stack(jnp.split(second, lax.axis_size("layer"), axis=3)), "layer", 0, 0),
+        axis=2,
+    )
     third = (
         lax.psum_scatter(
             product(left_second).astype(jnp.bfloat16), "layer", scatter_dimension=2, tiled=True

time: 2250 us -> 2150 us (0.956)
  local copies, waits for them, and re-layouts: 707 us -> 587 us
    concatenate x22 -> x13, local copies, waits for them, and re-layouts: 359 us -> 184 us  [product(): jnp.concatenate([left_tiles[left_index] for left_index, right_index in pa...]
    squeeze x0 -> x20, local copies, waits for them, and re-layouts: none -> 75.1 us  [product(): left_tiles[left_index]]
    slice x28 -> x15, local copies, waits for them, and re-layouts: 134 us -> 71.3 us  [product(): left_tiles[left_index]]
    another operation x0 -> x2, local copies, waits for them, and re-layouts: none -> 45.1 us  [per_device(): jnp.stack(jnp.split(second, lax.axis_size('layer'), axis=3))]
    unnamed x155 -> x199, local copies, waits for them, and re-layouts: 79.8 us -> 107 us
    convert_element_type x1 -> x0, local copies, waits for them, and re-layouts: 24 us -> none  [per_device(): second = (lax.psum_scatter(product(left_first), 'layer', scatter_dimensio...]
where the time goes in v1:
time: 2150 us; the launch traced here: 2140 us
  waiting for transfers between devices  1060 us (49%)
  local copies, waits for them, and re-layouts  587 us (27%)
  starting transfers between devices  179 us (8%)
  matrix products  142 us (7%)
  blocking collectives  83.2 us (4%)
  other arithmetic  66.4 us (3%)
    reduce_scatter x1, waiting for transfers between devices, per_device(): lax.psum_scatter(product(left_first), 'layer', scatter_dimension=2, tiled...  457 us
    ppermute x12, waiting for transfers between devices, passed_along(): return lax.ppermute(block, axis, route)  367 us
    reduce_scatter x1, waiting for transfers between devices, per_device(): lax.psum_scatter(product(left_second).astype(jnp.bfloat16), 'layer', scat...  238 us
    concatenate x13, local copies, waits for them, and re-layouts, product(): jnp.concatenate([left_tiles[left_index] for left_index, right_index in pa...  184 us
    ppermute x12, starting transfers between devices, passed_along(): return lax.ppermute(block, axis, route)  169 us
    dot_general x26, matrix products, product(): jnp.einsum('ixk,iky->ixy', lefts, rights, preferred_element_type=jnp.floa...  142 us
    unnamed x199, local copies, waits for them, and re-layouts  107 us
    all_to_all x1, blocking collectives, per_device(): lax.all_to_all(jnp.stack(jnp.split(second, lax.axis_size('layer'), axis=3...  83.2 us
  transfers between devices with their start and end apart: 17, of which 7 were waited for; matrix products, arithmetic and copies ran while one was open for 5% of the time, Pallas kernels for 0%

profile of v1, /device:TPU:0, one launch (start us, length us, event | category | flops | bytes accessed | tf_op | source)
XLA Modules:
  0.0 2135.4 jit_solution(11657083775965040314)
XLA Ops:
  7.9 6.6 broadcast_multiply_fusion
  14.5 24.0 %copy.291 = bf16[13,64,32,128]{1,2,0,3:T(8,128)(2,1)} copy(bf16[13,64,32,128]{3,2,1,0:T(8,128)(2,1)} %broadcast_multiply_fusion) | data formatting | bytes 13631488 | tf_op jit(solution)/shard_map/mul | solution.py:65
  38.5 13.8 reshape.124
  52.3 5.4 all-to-all-start
  79.5 5.7 gather_fusion.5
  105.4 5.9 gather_fusion
  134.3 112.0 %collective-permute-done.10 = bf16[6,31,32,128]{3,2,1,0:T(8,128)(2,1)} collective-permute-done((bf16[6,31,32,128]{3,2,1,0:T(8,128)(2,1)}, bf16[6,31,32,128]{3,2,1,0:T(8,128)(2,1)}, u32[]{:S(2)}, u32[]{:S(2)}) %collective-permute-start.10) | collective-permute-done | bytes 1523744 | tf_op jit(solution)/shard_map/ppermute | solution.py:15
  246.3 32.9 %collective-permute-start.4 = (bf16[6,33,32,128]{3,2,1,0:T(8,128)(2,1)S(1)}, bf16[6,33,32,128]{3,2,1,0:T(8,128)(2,1)S(1)}, u32[]{:S(2)}, u32[]{:S(2)}) collective-permute-start(bf16[6,33,32,128]{3,2,1,0:T(8,128)(2,1)S(1)} %copy-done.52), channel_id=1, source_target_pairs={{5,0},{6,1},{7,2},{0,3},{1,4},{2,5},{3,6},{4,7},{13,8},{14,9},{15,... | collective-permute-start | bytes 4866056 | tf_op jit(solution)/shard_map/ppermute | solution.py:15
  294.4 120.7 %collective-permute-start.2 = (bf16[6,33,32,128]{3,2,1,0:T(8,128)(2,1)S(1)}, bf16[6,33,32,128]{3,2,1,0:T(8,128)(2,1)}, u32[]{:S(2)}, u32[]{:S(2)}) collective-permute-start(bf16[6,33,32,128]{3,2,1,0:T(8,128)(2,1)S(1)} %slice.876), channel_id=1, source_target_pairs={{2,0},{3,1},{4,2},{5,3},{6,4},{7,5},{0,6},{1,7},{10,8},{11,9},{12,... | collective-permute-start | bytes 4866056 | tf_op jit(solution)/shard_map/ppermute | solution.py:15
  417.0 97.6 %collective-permute-done.9 = bf16[6,32,32,128]{3,2,1,0:T(8,128)(2,1)S(1)} collective-permute-done((bf16[6,32,32,128]{3,2,1,0:T(8,128)(2,1)S(1)}, bf16[6,32,32,128]{3,2,1,0:T(8,128)(2,1)S(1)}, u32[]{:S(2)}, u32[]{:S(2)}) %collective-permute-start.9) | collective-permute-done | bytes 1572896 | tf_op jit(solution)/shard_map/ppermute | solution.py:15
  523.1 93.9 %collective-permute-done.5 = bf16[6,31,32,128]{3,2,1,0:T(8,128)(2,1)} collective-permute-done((bf16[6,31,32,128]{3,2,1,0:T(8,128)(2,1)}, bf16[6,31,32,128]{3,2,1,0:T(8,128)(2,1)}, u32[]{:S(2)}, u32[]{:S(2)}) %collective-permute-start.5) | collective-permute-done | bytes 1523744 | tf_op jit(solution)/shard_map/ppermute | solution.py:15
  618.7 33.1 %collective-permute-done.2 = bf16[6,33,32,128]{3,2,1,0:T(8,128)(2,1)} collective-permute-done((bf16[6,33,32,128]{3,2,1,0:T(8,128)(2,1)S(1)}, bf16[6,33,32,128]{3,2,1,0:T(8,128)(2,1)}, u32[]{:S(2)}, u32[]{:S(2)}) %collective-permute-start.2) | collective-permute-done | bytes 1622048 | tf_op jit(solution)/shard_map/ppermute | solution.py:15
  655.7 30.6 %collective-permute-done.13 = bf16[6,33,32,128]{3,2,1,0:T(8,128)(2,1)S(1)} collective-permute-done((bf16[6,33,32,128]{3,2,1,0:T(8,128)(2,1)S(1)}, bf16[6,33,32,128]{3,2,1,0:T(8,128)(2,1)S(1)}, u32[]{:S(2)}, u32[]{:S(2)}) %collective-permute-start.13) | collective-permute-done | bytes 1622048 | tf_op jit(solution)/shard_map/ppermute | solution.py:15
  701.1 13.9 reshape.125
  715.0 13.1 copy.292
  728.2 4.9 fusion.136
  737.3 4.9 copy.295
  747.1 4.9 copy.293
  752.0 4.9 copy.297
  756.9 5.0 copy.298
  766.8 4.9 copy.301
  771.7 4.9 copy.302
  776.6 4.9 copy.303
  781.5 4.9 copy.305
  795.2 15.5 concatenate.198
  810.6 21.3 concatenate.203
  831.9 26.5 %concatenate.207 = bf16[64,128,416]{2,1,0:T(8,128)(2,1)} concatenate(bf16[64,128,32]{2,1,0:T(8,128)(2,1)} %bitcast.519, bf16[64,128,32]{2,1,0:T(8,128)(2,1)} %bitcast.464, bf16[64,128,32]{2,1,0:T(8,128)(2,1)} %bitcast.447, bf16[64,128,32]{2,1,0:T(8,128)(2,1)S(1)} %bitcast.424, bf16[64,128,32]{2,1,0:T(8,128)(2,1)} %bitcast.437, bf16[64,128,32]{2,1,0:T(8,128)(2,1)} %bitcast.456, ...), dimensions={2} | concatenate | bytes 13631488 | tf_op jit(solution)/shard_map/concatenate | solution.py:95
  858.5 21.3 concatenate.211
  879.7 15.5 concatenate.213
  895.3 13.6 concatenate.217
  908.8 13.2 concatenate.219
  922.0 13.2 concatenate.221
  935.3 13.2 concatenate.223
  948.5 13.2 concatenate.225
  961.7 13.3 concatenate.227
  975.0 8.0 bitcast_dynamic-update-slice_fusion.12
  983.0 5.5 bitcast_dynamic-update-slice_fusion.11
  988.5 8.3 bitcast_dynamic-update-slice_fusion.10
  996.8 7.4 bitcast_dynamic-update-slice_fusion.9
  1004.2 6.5 bitcast_dynamic-update-slice_fusion.8
  1010.7 5.6 bitcast_dynamic-update-slice_fusion.7
  1033.4 5.4 bitcast_dynamic-update-slice_fusion.2
  1038.8 5.2 bitcast_dynamic-update-slice_fusion.1
  1044.0 5.1 bitcast_dynamic-update-slice_fusion
  1049.2 457.4 %reduce-scatter.3.cloned.1.call-done = f32[13,64,32,128]{3,2,1,0:T(8,128)} async-done(((f32[13,64,128,128]{3,2,1,0:T(8,128)}), f32[13,64,32,128]{3,2,1,0:T(8,128)}) %reduce-scatter.3.cloned.1.call-update) | async-done | bytes 13631504 | tf_op jit(solution)/shard_map/reduce_scatter | solution.py:108
  1506.6 5.9 multiply_convert_fusion
  1512.5 11.3 slice_bitcast_fusion.3
  1523.9 19.0 pad_maximum_fusion
  1542.9 33.8 %copy.317 = bf16[4,13,64,32,32]{2,4,3,1,0:T(8,128)(2,1)} copy(bf16[4,13,64,32,32]{4,3,2,1,0:T(8,128)(2,1)} %pad_maximum_fusion) | data formatting | bytes 13631488 | tf_op jit(solution)/shard_map/stack | solution.py:112
  1576.7 13.8 reshape.126
  1590.5 83.2 %all_to_all.20 = bf16[4,2,425984]{2,1,0:T(2,128)(2,1)} all-to-all(bf16[4,2,425984]{2,1,0:T(2,128)(2,1)} %reshape.126), channel_id=1, replica_groups=mesh['layer'=4,'row'=2,'col'=4] {'layer'}, dimensions={0} | all-to-all | bytes 13631488 | tf_op jit(solution)/shard_map/all_to_all | solution.py:112
  1673.8 13.5 reshape.127
  1687.2 7.7 bitcast_bitcast_fusion
  1699.3 4.9 copy.321
  1724.8 5.0 copy.318
  1794.6 8.2 bitcast_dynamic-update-slice_fusion.25
  1812.6 6.1 bitcast_dynamic-update-slice_fusion.24
  1820.8 5.9 bitcast_dynamic-update-slice_fusion.23
  1828.9 8.9 bitcast_dynamic-update-slice_fusion.22
  1837.8 7.5 bitcast_dynamic-update-slice_fusion.21
  1845.3 5.0 bitcast_dynamic-update-slice_fusion.20
  1850.3 6.5 bitcast_dynamic-update-slice_fusion.19
  1879.4 238.3 %reduce-scatter.5.cloned.1.call-done = bf16[13,64,32,128]{3,2,1,0:T(8,128)(2,1)} async-done(((bf16[13,64,128,128]{3,2,1,0:T(8,128)(2,1)}), bf16[13,64,32,128]{3,2,1,0:T(8,128)(2,1)}) %reduce-scatter.5.cloned.1.call-update) | async-done | bytes 6815760 | tf_op jit(solution)/shard_map/reduce_scatter | solution.py:116
  2117.7 10.7 subtract_convert_fusion
  (298 shorter events, 278.2 us)
Async XLA Ops:
  52.3 12.0 copy-start.77
  52.3 12.0 copy-start.78
  52.3 648.9 %all-to-all-start = ((bf16[4,2,425984]{2,1,0:T(2,128)(2,1)}), bf16[4,2,425984]{2,1,0:T(2,128)(2,1)}, u32[]{:S(2)}, u32[]{:S(2)}) async-start(bf16[4,2,425984]{2,1,0:T(2,128)(2,1)} %reshape.124), calls=%async_computation | async-start | bytes 13631488 | tf_op jit(solution)/shard_map/all_to_all | solution.py:106
  57.7 1448.9 %reduce-scatter.3.cloned.1.call-start = ((), (), s32[]{:S(2)}) async-start(), calls=%async_computation.4 | async-start | bytes 68157440 | tf_op jit(solution)/shard_map/reduce_scatter | solution.py:108
  59.8 67.5 %collective-permute-start.1 = (bf16[13,3,32,128]{3,2,1,0:T(8,128)(2,1)}, bf16[13,3,32,128]{3,2,1,0:T(8,128)(2,1)S(1)}, u32[]{:S(2)}, u32[]{:S(2)}) collective-permute-start(bf16[13,3,32,128]{3,2,1,0:T(8,128)(2,1)} %get-tuple-element.92), channel_id=1, source_target_pairs={{1,0},{2,1},{3,2},{4,3},{5,4},{6,5},{7,6},{0,7},{9,8},{10,9},{11,1... | collective-permute-start | bytes 958472 | tf_op jit(solution)/shard_map/ppermute | solution.py:27
  64.3 54.9 %collective-permute-start = (bf16[13,3,32,128]{3,2,1,0:T(8,128)(2,1)}, bf16[13,3,32,128]{3,2,1,0:T(8,128)(2,1)}, u32[]{:S(2)}, u32[]{:S(2)}) collective-permute-start(bf16[13,3,32,128]{3,2,1,0:T(8,128)(2,1)} %get-tuple-element.93), channel_id=1, source_target_pairs={{0,1},{1,2},{2,3},{3,4},{4,5},{5,6},{6,7},{7,0},{8,9},{9,10},{10,1... | collective-permute-start | bytes 958472 | tf_op jit(solution)/shard_map/ppermute | solution.py:24
  70.8 216.7 %collective-permute-start.6 = (bf16[6,32,32,128]{3,2,1,0:T(8,128)(2,1)}, bf16[6,32,32,128]{3,2,1,0:T(8,128)(2,1)}, u32[]{:S(2)}, u32[]{:S(2)}) collective-permute-start(bf16[6,32,32,128]{3,2,1,0:T(8,128)(2,1)} %get-tuple-element.133), channel_id=1, source_target_pairs={{2,0},{3,1},{4,2},{5,3},{6,4},{7,5},{0,6},{1,7},{10,8},{11,9},{12,... | collective-permute-start | bytes 4718600 | tf_op jit(solution)/shard_map/ppermute | solution.py:15
  75.3 9.8 copy-start.25
  77.0 169.2 %collective-permute-start.10 = (bf16[6,31,32,128]{3,2,1,0:T(8,128)(2,1)}, bf16[6,31,32,128]{3,2,1,0:T(8,128)(2,1)}, u32[]{:S(2)}, u32[]{:S(2)}) collective-permute-start(bf16[6,31,32,128]{3,2,1,0:T(8,128)(2,1)} %slice.922), channel_id=1, source_target_pairs={{2,0},{3,1},{4,2},{5,3},{6,4},{7,5},{0,6},{1,7},{10,8},{11,9},{12,... | collective-permute-start | bytes 4571144 | tf_op jit(solution)/shard_map/ppermute | solution.py:15
  88.0 191.1 %collective-permute-start.12 = (bf16[6,31,32,128]{3,2,1,0:T(8,128)(2,1)}, bf16[6,31,32,128]{3,2,1,0:T(8,128)(2,1)}, u32[]{:S(2)}, u32[]{:S(2)}) collective-permute-start(bf16[6,31,32,128]{3,2,1,0:T(8,128)(2,1)} %slice.927), channel_id=1, source_target_pairs={{5,0},{6,1},{7,2},{0,3},{1,4},{2,5},{3,6},{4,7},{13,8},{14,9},{15,... | collective-permute-start | bytes 4571144 | tf_op jit(solution)/shard_map/ppermute | solution.py:15
  105.4 12.9 slice-start
  111.3 6.7 copy-start.26
  111.3 7.1 slice-start.1
  119.2 175.2 %collective-permute-start.7 = (bf16[6,32,32,128]{3,2,1,0:T(8,128)(2,1)S(1)}, bf16[6,32,32,128]{3,2,1,0:T(8,128)(2,1)S(1)}, u32[]{:S(2)}, u32[]{:S(2)}) collective-permute-start(bf16[6,32,32,128]{3,2,1,0:T(8,128)(2,1)S(1)} %copy-done.59), channel_id=1, source_target_pairs={{3,0},{4,1},{5,2},{6,3},{7,4},{0,5},{1,6},{2,7},{11,8},{12,9},{13,... | collective-permute-start | bytes 4718600 | tf_op jit(solution)/shard_map/ppermute | solution.py:15
  127.3 287.8 %collective-permute-start.8 = (bf16[6,32,32,128]{3,2,1,0:T(8,128)(2,1)S(1)}, bf16[6,32,32,128]{3,2,1,0:T(8,128)(2,1)S(1)}, u32[]{:S(2)}, u32[]{:S(2)}) collective-permute-start(bf16[6,32,32,128]{3,2,1,0:T(8,128)(2,1)S(1)} %copy-done.61), channel_id=1, source_target_pairs={{5,0},{6,1},{7,2},{0,3},{1,4},{2,5},{3,6},{4,7},{13,8},{14,9},{15,... | collective-permute-start | bytes 4718600 | tf_op jit(solution)/shard_map/ppermute | solution.py:15
  131.2 115.1 %copy-start.52 = (bf16[6,33,32,128]{3,2,1,0:T(8,128)(2,1)S(1)}, bf16[6,33,32,128]{3,2,1,0:T(8,128)(2,1)}, u32[]{:S(2)}) copy-start(bf16[6,33,32,128]{3,2,1,0:T(8,128)(2,1)} %slice.879) | copy-start | bytes 4866052
  131.2 147.9 %copy-start.60 = (bf16[6,32,32,128]{3,2,1,0:T(8,128)(2,1)S(1)}, bf16[6,32,32,128]{3,2,1,0:T(8,128)(2,1)}, u32[]{:S(2)}) copy-start(bf16[6,32,32,128]{3,2,1,0:T(8,128)(2,1)} %get-tuple-element.130) | copy-start | bytes 4718596
  246.3 269.5 %collective-permute-start.4 = (bf16[6,33,32,128]{3,2,1,0:T(8,128)(2,1)S(1)}, bf16[6,33,32,128]{3,2,1,0:T(8,128)(2,1)S(1)}, u32[]{:S(2)}, u32[]{:S(2)}) collective-permute-start(bf16[6,33,32,128]{3,2,1,0:T(8,128)(2,1)S(1)} %copy-done.52), channel_id=1, source_target_pairs={{5,0},{6,1},{7,2},{0,3},{1,4},{2,5},{3,6},{4,7},{13,8},{14,9},{15,... | collective-permute-start | bytes 4866056 | tf_op jit(solution)/shard_map/ppermute | solution.py:15
  279.1 235.5 %collective-permute-start.9 = (bf16[6,32,32,128]{3,2,1,0:T(8,128)(2,1)S(1)}, bf16[6,32,32,128]{3,2,1,0:T(8,128)(2,1)S(1)}, u32[]{:S(2)}, u32[]{:S(2)}) collective-permute-start(bf16[6,32,32,128]{3,2,1,0:T(8,128)(2,1)S(1)} %copy-done.60), channel_id=1, source_target_pairs={{6,0},{7,1},{0,2},{1,3},{2,4},{3,5},{4,6},{5,7},{14,8},{15,9},{8,1... | collective-permute-start | bytes 4718600 | tf_op jit(solution)/shard_map/ppermute | solution.py:15
  287.5 329.4 %collective-permute-start.5 = (bf16[6,31,32,128]{3,2,1,0:T(8,128)(2,1)}, bf16[6,31,32,128]{3,2,1,0:T(8,128)(2,1)}, u32[]{:S(2)}, u32[]{:S(2)}) collective-permute-start(bf16[6,31,32,128]{3,2,1,0:T(8,128)(2,1)} %slice.880), channel_id=1, source_target_pairs={{6,0},{7,1},{0,2},{1,3},{2,4},{3,5},{4,6},{5,7},{14,8},{15,9},{8,1... | collective-permute-start | bytes 4571144 | tf_op jit(solution)/shard_map/ppermute | solution.py:15
  294.4 122.6 %copy-start.53 = (bf16[6,32,32,128]{3,2,1,0:T(8,128)(2,1)}, bf16[6,32,32,128]{3,2,1,0:T(8,128)(2,1)S(1)}, u32[]{:S(2)}) copy-start(bf16[6,32,32,128]{3,2,1,0:T(8,128)(2,1)S(1)} %collective-permute-done.7) | copy-start | bytes 4718596
  294.4 357.3 %collective-permute-start.2 = (bf16[6,33,32,128]{3,2,1,0:T(8,128)(2,1)S(1)}, bf16[6,33,32,128]{3,2,1,0:T(8,128)(2,1)}, u32[]{:S(2)}, u32[]{:S(2)}) collective-permute-start(bf16[6,33,32,128]{3,2,1,0:T(8,128)(2,1)S(1)} %slice.876), channel_id=1, source_target_pairs={{2,0},{3,1},{4,2},{5,3},{6,4},{7,5},{0,6},{1,7},{10,8},{11,9},{12,... | collective-permute-start | bytes 4866056 | tf_op jit(solution)/shard_map/ppermute | solution.py:15
  415.1 238.4 %collective-permute-start.3 = (bf16[6,31,32,128]{3,2,1,0:T(8,128)(2,1)}, bf16[6,31,32,128]{3,2,1,0:T(8,128)(2,1)}, u32[]{:S(2)}, u32[]{:S(2)}) collective-permute-start(bf16[6,31,32,128]{3,2,1,0:T(8,128)(2,1)} %slice.877), channel_id=1, source_target_pairs={{3,0},{4,1},{5,2},{6,3},{7,4},{0,5},{1,6},{2,7},{11,8},{12,9},{13,... | collective-permute-start | bytes 4571144 | tf_op jit(solution)/shard_map/ppermute | solution.py:15
  514.7 140.6 %collective-permute-start.11 = (bf16[6,33,32,128]{3,2,1,0:T(8,128)(2,1)S(1)}, bf16[6,33,32,128]{3,2,1,0:T(8,128)(2,1)S(1)}, u32[]{:S(2)}, u32[]{:S(2)}) collective-permute-start(bf16[6,33,32,128]{3,2,1,0:T(8,128)(2,1)S(1)} %slice.923), channel_id=1, source_target_pairs={{3,0},{4,1},{5,2},{6,3},{7,4},{0,5},{1,6},{2,7},{11,8},{12,9},{13,... | collective-permute-start | bytes 4866056 | tf_op jit(solution)/shard_map/ppermute | solution.py:15
  515.8 5.8 copy-start.56
  515.8 170.6 %collective-permute-start.13 = (bf16[6,33,32,128]{3,2,1,0:T(8,128)(2,1)S(1)}, bf16[6,33,32,128]{3,2,1,0:T(8,128)(2,1)S(1)}, u32[]{:S(2)}, u32[]{:S(2)}) collective-permute-start(bf16[6,33,32,128]{3,2,1,0:T(8,128)(2,1)S(1)} %slice.928), channel_id=1, source_target_pairs={{6,0},{7,1},{0,2},{1,3},{2,4},{3,5},{4,6},{5,7},{14,8},{15,9},{8,1... | collective-permute-start | bytes 4866056 | tf_op jit(solution)/shard_map/ppermute | solution.py:15
  693.2 5.6 copy-start.11
  693.2 5.6 copy-start.14
  693.2 5.6 copy-start.17
  961.7 13.3 copy-start.69
  961.7 13.3 copy-start.70
  975.0 8.0 copy-start.4
  983.0 13.8 slice-start.2
  988.5 8.3 slice-start.3
  988.5 15.7 slice-start.4
  996.8 7.4 slice-start.5
  1004.2 6.5 copy-start.3
  1010.6 5.6 copy-start
  1010.6 5.6 copy-start.1
  1010.6 5.6 copy-start.2
  1010.6 5.6 copy-start.62
  1010.7 5.6 copy-start.64
  1010.7 5.6 copy-start.66
  1010.7 5.6 copy-start.68
  1033.4 5.4 copy-start.6
  1038.8 5.2 copy-start.5
  1049.1 457.5 %copy-start.71 = (f32[13,64]{1,0:T(8,128)S(1)}, f32[13,64]{1,0:T(8,128)}, u32[]{:S(2)}) copy-start(f32[13,64]{1,0:T(8,128)} %get-tuple-element.208) | copy-start | bytes 9988
  1049.2 1068.5 %reduce-scatter.5.cloned.1.call-start = ((), (), s32[]{:S(2)}) async-start(), calls=%async_computation.5 | async-start | bytes 34078720 | tf_op jit(solution)/shard_map/reduce_scatter | solution.py:116
  1742.0 10.4 copy-start.49
  1745.9 6.8 copy-start.48
  1748.2 5.1 copy-start.51
  1756.1 9.8 copy-start.34
  1761.1 5.9 copy-start.35
  1794.6 8.2 copy-start.46
  1794.6 9.7 copy-start.21
  1794.6 9.7 copy-start.24
  1794.6 9.7 copy-start.43
  1812.6 6.1 copy-start.33
  1812.6 6.1 copy-start.38
  1820.7 5.9 copy-start.37
  1837.8 7.5 copy-start.36
  1845.2 5.0 copy-start.65
  1850.3 6.6 copy-start.19
  1879.3 238.4 %copy-start.72 = (f32[13,64]{1,0:T(8,128)S(1)}, f32[13,64]{1,0:T(8,128)}, u32[]{:S(2)}) copy-start(f32[13,64]{1,0:T(8,128)} %get-tuple-element.208) | copy-start | bytes 9988
  (38 other events, 128.7 us)
Sparse Core Ops, SparseCore 0:
  1049.3 457.2 reduce-scatter.2
  1879.5 238.1 reduce-scatter.4
